TPU v7x, 256 devices: a whole 4x4x8 slice. The times are simulated.
256 devices in a mesh: ctx: 32 (over y, z), head: 8 (over x, core).
Axes of the slice: x: 4, y: 4, z: 8, core: 2. Of those that a mesh axis runs over, the one named last changes fastest.
Arguments:
- mixer_input: bfloat16 [32768, 8192], P(('ctx', 'head')), may hold values from -0.0625 to 0.0625
- write_vectors: bfloat16 [32768, 1024], P(('ctx', 'head')), may hold values from -0.1875 to 0.1875
- read_vectors: bfloat16 [32768, 1024], P(('ctx', 'head')), may hold values from -0.1875 to 0.1875
- step_sizes: bfloat16 [32768, 128], P(('ctx', 'head')), may hold values from 0.5 to 22937
- fast_rates: float32 [128], replicated, may hold values from 1.5258789e-06 to 0.034
- slow_heads: int32 [64], replicated, may hold values from 0 to 127, as said below
- skip_gains: float32 [128], replicated, may hold values from 0.5 to 1.5
- mixer_grad: bfloat16 [32768, 8192], P(('ctx', 'head')), may hold values from -6 to 6
- queries: bfloat16 [32768, 4096], P(('ctx', 'head')), may hold values from -150 to 150
- attn_keys: bfloat16 [32768, 1024], P(('ctx', 'head')), may hold values from -6 to 6
- attn_values: bfloat16 [32768, 1024], P(('ctx', 'head')), may hold values from -24 to 24
- attn_grad: bfloat16 [32768, 4096], P(('ctx', 'head')), may hold values from -24 to 24
- doc_lengths: int32 [16], replicated, may hold values from 1 to 3072, 32768 in all
Outputs:
- grad_mixer_input: bfloat16 [32768, 8192], P(('ctx', 'head'))
- grad_write: bfloat16 [32768, 1024], P(('ctx', 'head'))
- grad_read: bfloat16 [32768, 1024], P(('ctx', 'head'))
- grad_queries: bfloat16 [32768, 4096], P(('ctx', 'head'))
Inputs may be any that keep to these rules, and one draw needn't show every extreme that they name: `slow_heads`: distinct head numbers.
All inputs are finite; a program needn't handle non-finite values.
Results may differ from a plain program's by a relative error of at most 0.0062.
Values may be sent and summed in bfloat16 or wider, within the bound.
A program may use at most 192 MiB of HBM per device.

v0:
```python
import jax
import jax.numpy as jnp
from jax import lax
from jax.sharding import Mesh
from jax.sharding import PartitionSpec as P

MH = 128
HD = 64
NS = 128
DH = 128
BLOCK = 256
CTX = ("ctx_0", "ctx_1")
CTX_HEAD = ("ctx_0", "ctx_1", "head")
slab_reach = 3


def filled_with(shard, identity):
    return jax.tree.map(
        lambda a, e: jnp.broadcast_to(jnp.asarray(e, a.dtype), a.shape), shard, identity
    )


def entering_2(shard, axes, combine, identity, reverse):
    before = start = filled_with(shard, identity)
    so_far = shard
    for axis in reversed(axes):
        devices, position = (lax.axis_size(axis), lax.axis_index(axis))
        pieces = jax.tree.map(lambda part: lax.all_gather(part, axis), so_far)
        inside, so_far = (start, start)
        for k in reversed(range(devices)) if reverse else range(devices):
            passed = k > position if reverse else k < position
            so_far = combine(so_far, jax.tree.map(lambda part: part[k], pieces))
            inside = jax.tree.map(lambda new, old: jnp.where(passed, new, old), so_far, inside)
        before = combine(inside, before)
    return before


def from_behind(value, axis, steps):
    count = lax.axis_size(axis)
    leading, last = (max(0, -steps), min(count, count - steps))
    return lax.ppermute(value, axis, [(source, source + steps) for source in range(leading, last)])


def doc_index(positions, doc_lengths):
    starts = jnp.cumsum(doc_lengths) - doc_lengths
    match_count = (starts[None, :] <= positions[:, None]).astype(jnp.int32)
    return jnp.sum(match_count, axis=1) - 1


def combine(earlier, latter):
    factor = latter[0]
    return (earlier[0] * factor, factor[..., None, None] * earlier[1] + latter[1])


def stretch_edges(
    stretch_inputs, stretch_write, stretch_read, decay_log, stretch_grads, docs, doc_prev
):
    cumulative = jnp.cumsum(decay_log, axis=1)
    totals = cumulative[:, -1]
    linked = (docs == doc_prev[:, None]).astype(jnp.float32)
    tail_doc = (docs == docs[:, -1:]).astype(jnp.float32)
    stretch_links = jnp.exp(totals) * linked[:, -1][:, None, None]
    entering = jnp.exp(cumulative) * linked[:, :, None, None]
    to_end = jnp.exp(totals[:, None] - cumulative) * tail_doc[:, :, None, None]
    input_weighted = (stretch_inputs.astype(jnp.float32) * to_end[..., None]).astype(jnp.bfloat16)
    grad_weighted = (stretch_grads.astype(jnp.float32) * entering[..., None]).astype(jnp.bfloat16)
    endings = jnp.einsum(
        "ksghp,ksgn->kghpn", input_weighted, stretch_write, preferred_element_type=jnp.float32
    )
    openings = jnp.einsum(
        "ktghp,ktgn->kghpn", grad_weighted, stretch_read, preferred_element_type=jnp.float32
    )
    return (cumulative, stretch_links, to_end, input_weighted, grad_weighted, endings, openings)


def stretch_inner(stretch_inputs, stretch_write, stretch_read, stretch_grads, docs, cumulative):
    block_rows = stretch_inputs.shape[1]
    offsets = jnp.arange(block_rows, dtype=jnp.int32)
    causal = offsets[:, None] >= offsets[None, :]
    same_doc = causal[None] & (docs[:, :, None] == docs[:, None, :])
    cum_heads = jnp.transpose(cumulative, (0, 2, 3, 1))
    log_gaps = cum_heads[..., :, None] - cum_heads[..., None, :]
    decays = jnp.exp(jnp.where(same_doc[:, None, None], log_gaps, -jnp.inf))
    scores = jnp.einsum(
        "ktgn,ksgn->kgts", stretch_read, stretch_write, preferred_element_type=jnp.float32
    )
    mixing = (scores[:, :, None] * decays).astype(jnp.bfloat16)
    input_inner = jnp.einsum(
        "kghts,ktghp->ksghp", mixing, stretch_grads, preferred_element_type=jnp.float32
    )
    inner_products = jnp.einsum(
        "ktghp,ksghp->kghts", stretch_grads, stretch_inputs, preferred_element_type=jnp.float32
    )
    joint_weights = jnp.sum(inner_products * decays, axis=2).astype(jnp.bfloat16)
    read_inner = jnp.einsum(
        "kgts,ksgn->ktgn", joint_weights, stretch_write, preferred_element_type=jnp.float32
    )
    write_inner = jnp.einsum(
        "kgts,ktgn->ksgn", joint_weights, stretch_read, preferred_element_type=jnp.float32
    )
    return (input_inner, write_inner, read_inner)


def mixer_grads(
    inputs_here,
    write_here,
    read_here,
    steps_here,
    grad_here,
    fast_rates,
    slow_heads,
    skip_gains,
    doc_lengths,
    first_row,
    head_index,
    total_rows,
):
    row_count = inputs_here.shape[0]
    local_heads = steps_here.shape[1]
    local_groups = write_here.shape[1] // NS
    per_group = local_heads // local_groups
    stretch_count = row_count // BLOCK
    head_ids = jnp.arange(MH, dtype=jnp.int32)
    slow_mask = jnp.any(head_ids[:, None] == slow_heads[None, :], axis=1)
    rates = jnp.where(slow_mask, 1.0 / total_rows, fast_rates)
    head_start = head_index * local_heads
    rates_here = lax.dynamic_slice_in_dim(rates, head_start, local_heads).reshape(
        local_groups, per_group
    )
    skips_here = lax.dynamic_slice_in_dim(skip_gains, head_start, local_heads).reshape(
        local_groups, per_group
    )
    decay_log = (
        -steps_here.astype(jnp.float32).reshape(stretch_count, BLOCK, local_groups, per_group)
        * rates_here
    )
    shape_x = (stretch_count, BLOCK, local_groups, per_group, HD)
    shape_v = (stretch_count, BLOCK, local_groups, NS)
    stretch_inputs = inputs_here.reshape(shape_x)
    stretch_grads = grad_here.reshape(shape_x)
    stretch_write = write_here.reshape(shape_v)
    stretch_read = read_here.reshape(shape_v)
    positions = first_row + jnp.arange(row_count, dtype=jnp.int32)
    docs = doc_index(positions, doc_lengths).reshape(stretch_count, BLOCK)
    doc_prev = doc_index(
        first_row - 1 + BLOCK * jnp.arange(stretch_count, dtype=jnp.int32), doc_lengths
    )
    cumulative, stretch_links, to_end, input_weighted, grad_weighted, endings, openings = (
        stretch_edges(
            stretch_inputs, stretch_write, stretch_read, decay_log, stretch_grads, docs, doc_prev
        )
    )
    input_inner, write_inner, read_inner = stretch_inner(
        stretch_inputs, stretch_write, stretch_read, stretch_grads, docs, cumulative
    )

    def forward_local(carried, element):
        stretch_link, ending = element
        return (
            (stretch_link[..., None, None] * carried[0] + ending, stretch_link * carried[1]),
            carried,
        )

    def backward_local(carried, element):
        stretch_link, opening = element
        return (
            (opening + stretch_link[..., None, None] * carried[0], stretch_link * carried[1]),
            carried,
        )

    zero_state = jnp.zeros_like(endings[0])
    unit_links = jnp.ones_like(stretch_links[0])
    (device_end, device_link), (local_states, local_links) = lax.scan(
        forward_local, (zero_state, unit_links), (stretch_links, endings)
    )
    (device_open, unused), (local_backs, back_links) = lax.scan(
        backward_local, (zero_state, unit_links), (stretch_links, openings), reverse=True
    )
    state_in = entering_2((device_link, device_end), CTX, combine, (unit_links, zero_state), False)[
        1
    ]
    back_out = entering_2((device_link, device_open), CTX, combine, (unit_links, zero_state), True)[
        1
    ]
    states_low = (local_states + local_links[..., None, None] * state_in).astype(jnp.bfloat16)
    backs_low = (local_backs + back_links[..., None, None] * back_out).astype(jnp.bfloat16)
    read_carried = jnp.einsum(
        "ktghp,kghpn->ktgn", grad_weighted, states_low, preferred_element_type=jnp.float32
    )
    write_carried = jnp.einsum(
        "ksghp,kghpn->ksgn", input_weighted, backs_low, preferred_element_type=jnp.float32
    )
    input_carried = to_end[..., None] * jnp.einsum(
        "ksgn,kghpn->ksghp", stretch_write, backs_low, preferred_element_type=jnp.float32
    )
    grad_input = (
        input_inner + input_carried + skips_here[..., None] * stretch_grads.astype(jnp.float32)
    ).astype(jnp.bfloat16)
    grad_write = (write_inner + write_carried).astype(jnp.bfloat16)
    grad_read = (read_inner + read_carried).astype(jnp.bfloat16)
    return (
        grad_input.reshape(row_count, -1),
        grad_write.reshape(row_count, -1),
        grad_read.reshape(row_count, -1),
    )


def attend_block(
    query_block, grad_block, key_block, value_block, query_pos, key_pos, query_doc, key_doc
):
    scaling = query_block.shape[-1] ** (-0.5)
    logits = (
        jnp.einsum("qrd,kd->rqk", query_block, key_block, preferred_element_type=jnp.float32)
        * scaling
    )
    allowed = (
        (key_pos[None, :] <= query_pos[:, None])
        & (key_pos[None, :] >= 0)
        & (query_doc[:, None] == key_doc[None, :])
    )
    logits = jnp.where(allowed, logits, -jnp.inf)
    row_peaks = jnp.max(logits, axis=-1, keepdims=True)
    weights = jnp.exp(logits - row_peaks)
    probabilities = weights / jnp.sum(weights, axis=-1, keepdims=True)
    grad_probs = jnp.einsum(
        "qrd,kd->rqk", grad_block, value_block, preferred_element_type=jnp.float32
    )
    centre = jnp.sum(probabilities * grad_probs, axis=-1, keepdims=True)
    grad_logits = (probabilities * (grad_probs - centre)).astype(jnp.bfloat16)
    return (
        jnp.einsum("rqk,kd->qrd", grad_logits, key_block, preferred_element_type=jnp.float32)
        * scaling
    )


def attend(
    query_rows, grad_rows, key_rows, value_rows, first_row, lead_rows, doc_reach, doc_lengths
):
    row_count = query_rows.shape[0]
    kv_heads = key_rows.shape[1] // DH
    group_size = query_rows.shape[1] // key_rows.shape[1]
    query_four = query_rows.reshape(row_count, kv_heads, group_size, DH)
    grad_four = grad_rows.reshape(row_count, kv_heads, group_size, DH)
    key_three = key_rows.reshape(-1, kv_heads, DH)
    value_three = value_rows.reshape(-1, kv_heads, DH)
    block_rows = min(128, row_count)
    block_count = row_count // block_rows
    span = doc_reach + block_rows
    query_positions = first_row + jnp.arange(row_count, dtype=jnp.int32)
    key_positions = first_row - lead_rows + jnp.arange(key_rows.shape[0], dtype=jnp.int32)
    query_docs = doc_index(query_positions, doc_lengths)
    key_docs = doc_index(key_positions, doc_lengths)

    def one_item(index):
        block = index // kv_heads
        which = index % kv_heads
        begin = block * block_rows
        key_begin = begin + lead_rows - doc_reach
        query_part = lax.dynamic_index_in_dim(
            lax.dynamic_slice_in_dim(query_four, begin, block_rows, 0), which, 1, keepdims=False
        )
        grad_part = lax.dynamic_index_in_dim(
            lax.dynamic_slice_in_dim(grad_four, begin, block_rows, 0), which, 1, keepdims=False
        )
        key_part = lax.dynamic_index_in_dim(
            lax.dynamic_slice_in_dim(key_three, key_begin, span, 0), which, 1, keepdims=False
        )
        value_part = lax.dynamic_index_in_dim(
            lax.dynamic_slice_in_dim(value_three, key_begin, span, 0), which, 1, keepdims=False
        )
        return attend_block(
            query_part,
            grad_part,
            key_part,
            value_part,
            lax.dynamic_slice_in_dim(query_positions, begin, block_rows, 0),
            lax.dynamic_slice_in_dim(key_positions, key_begin, span, 0),
            lax.dynamic_slice_in_dim(query_docs, begin, block_rows, 0),
            lax.dynamic_slice_in_dim(key_docs, key_begin, span, 0),
        )

    items = lax.map(one_item, jnp.arange(block_count * kv_heads, dtype=jnp.int32))
    items = items.reshape(block_count, kv_heads, block_rows, group_size, DH).transpose(
        0, 2, 1, 3, 4
    )
    return items.reshape(row_count, -1).astype(jnp.bfloat16)


def head_attention(query_rows, key_rows, value_rows, grad_rows, doc_lengths, first_row):
    row_count = query_rows.shape[0]
    earlier_keys = []
    earlier_values = []
    for distance in range(slab_reach, 0, -1):
        fetched = from_behind((key_rows, value_rows), CTX, distance)
        earlier_keys.append(fetched[0])
        earlier_values.append(fetched[1])
    key_all = jnp.concatenate(earlier_keys + [key_rows], axis=0)
    value_all = jnp.concatenate(earlier_values + [value_rows], axis=0)
    lead = slab_reach * row_count
    return attend(query_rows, grad_rows, key_all, value_all, first_row, lead, lead, doc_lengths)


def shards(
    mixer_input,
    write_vectors,
    read_vectors,
    step_sizes,
    fast_rates,
    slow_heads,
    skip_gains,
    mixer_grad,
    queries,
    attn_keys,
    attn_values,
    attn_grad,
    doc_lengths,
):
    head_count = lax.axis_size("head")
    ctx_index = lax.axis_index(CTX)
    head_index = lax.axis_index("head")
    shard_rows = mixer_input.shape[0] * head_count
    total_rows = shard_rows * lax.axis_size(CTX)
    moved = (
        lax.all_to_all(mixer_input, "head", split_axis=1, concat_axis=0, tiled=True),
        lax.all_to_all(write_vectors, "head", split_axis=1, concat_axis=0, tiled=True),
        lax.all_to_all(read_vectors, "head", split_axis=1, concat_axis=0, tiled=True),
        lax.all_to_all(step_sizes, "head", split_axis=1, concat_axis=0, tiled=True),
        lax.all_to_all(mixer_grad, "head", split_axis=1, concat_axis=0, tiled=True),
        lax.all_to_all(queries, "head", split_axis=1, concat_axis=0, tiled=True),
        lax.all_to_all(attn_keys, "head", split_axis=1, concat_axis=0, tiled=True),
        lax.all_to_all(attn_values, "head", split_axis=1, concat_axis=0, tiled=True),
        lax.all_to_all(attn_grad, "head", split_axis=1, concat_axis=0, tiled=True),
    )
    grad_query_heads = head_attention(
        moved[5], moved[6], moved[7], moved[8], doc_lengths, ctx_index * shard_rows
    )
    grad_input, grad_write, grad_read = mixer_grads(
        moved[0],
        moved[1],
        moved[2],
        moved[3],
        moved[4],
        fast_rates,
        slow_heads,
        skip_gains,
        doc_lengths,
        ctx_index * shard_rows,
        head_index,
        total_rows,
    )
    returned = (
        lax.all_to_all(grad_input, "head", split_axis=0, concat_axis=1, tiled=True),
        lax.all_to_all(grad_write, "head", split_axis=0, concat_axis=1, tiled=True),
        lax.all_to_all(grad_read, "head", split_axis=0, concat_axis=1, tiled=True),
        lax.all_to_all(grad_query_heads, "head", split_axis=0, concat_axis=1, tiled=True),
    )
    return (returned[0], returned[1], returned[2], returned[3])


def solution(mesh):
    split = Mesh(mesh.devices.reshape(4, 8, mesh.shape["head"]), ("ctx_0", "ctx_1", "head"))
    return jax.shard_map(
        shards,
        mesh=split,
        in_specs=(
            P(CTX_HEAD, None),
            P(CTX_HEAD, None),
            P(CTX_HEAD, None),
            P(CTX_HEAD, None),
            P(),
            P(),
            P(),
            P(CTX_HEAD, None),
            P(CTX_HEAD, None),
            P(CTX_HEAD, None),
            P(CTX_HEAD, None),
            P(CTX_HEAD, None),
            P(),
        ),
        out_specs=(P(CTX_HEAD, None), P(CTX_HEAD, None), P(CTX_HEAD, None), P(CTX_HEAD, None)),
        check_vma=False,
    )
```

profile of v0, /device:TPU:1, one launch (start us, length us, event | category | flops | bytes accessed | tf_op | source)
XLA Modules:
  0.0 617.0 jit_solution(6818892694384859744)
XLA Ops:
  32.0 22.2 %all-to-all-done.4 = bf16[128,8,1024]{0,2,1:T(8,128)(2,1)S(1)} async-done(((bf16[128,8,1024]{0,2,1:T(8,128)(2,1)}), bf16[128,8,1024]{0,2,1:T(8,128)(2,1)S(1)}, u32[]{:S(2)}, u32[]{:S(2)}) %all-to-all-start.4) | async-done | bytes 2097184 | tf_op jit(solution)/shard_map/all_to_all | solution.py:324
  86.3 25.5 %all-to-all-done.3 = bf16[128,8,1024]{0,2,1:T(8,128)(2,1)S(1)} async-done(((bf16[128,8,1024]{0,2,1:T(8,128)(2,1)}), bf16[128,8,1024]{0,2,1:T(8,128)(2,1)S(1)}, u32[]{:S(2)}, u32[]{:S(2)}) %all-to-all-start.3) | async-done | bytes 2097184 | tf_op jit(solution)/shard_map/all_to_all | solution.py:328
  129.3 8.2 %while.53 = (s32[]{:T(128)}, f32[1,16,64,128]{3,2,1,0:T(8,128)S(1)}, f32[1,16]{1,0:T(1,128)S(1)}, f32[4,1,16,64,128]{4,3,2,1,0:T(8,128)}, f32[4,1,16]{2,1,0:T(1,...) while((s32[]{:T(128)}, ...), condition=%wide.region_7.8_spmd.clone, body=%wide.region_6.7_spmd.clone.sunk | while | flops 524340 | bytes 2622994 | solution.py:176
  138.4 14.6 %all-gather.3 = f32[8,1,16]{2,1,0:T(1,128)S(1)} all-gather(f32[1,1,16]{2,1,0:T(1,128)S(1)} %bitcast.562), channel_id=2, replica_groups=mesh['ctx_0'=4,'ctx_1'=8,'head'=8] {'ctx_1'}, dimensions={0}, use_global_device_ids=true | all-gather | bytes 576 | tf_op jit(solution)/shard_map/all_gather | solution.py:28
  159.4 8.6 %all-to-all-start.8 = ((bf16[128,8,128]{2,0,1:T(8,128)(2,1)}), bf16[128,8,128]{2,0,1:T(8,128)(2,1)}, u32[]{:S(2)}, u32[]{:S(2)}) async-start(bf16[128,8,128]{2,0,1:T(8,128)(2,1)} %copy_bitcast_fusion.3), calls=%async_computation.8 | async-start | bytes 524288 | tf_op jit(solution)/shard_map/all_to_all | solution.py:330
  236.0 13.2 %collective-permute-done.3 = bf16[1024,128]{1,0:T(8,128)(2,1)} collective-permute-done((bf16[1024,128]{1,0:T(8,128)(2,1)}, bf16[1024,128]{1,0:T(8,128)(2,1)}, u32[]{:S(2)}, u32[]{:S(2)}) %collective-permute-start.3) | collective-permute-done | bytes 262176 | tf_op jit(solution)/shard_map/ppermute | solution.py:41
  249.2 7.6 %collective-permute-done.4 = bf16[1024,128]{1,0:T(8,128)(2,1)} collective-permute-done((bf16[1024,128]{1,0:T(8,128)(2,1)}, bf16[1024,128]{1,0:T(8,128)(2,1)}, u32[]{:S(2)}, u32[]{:S(2)}) %collective-permute-start.4) | collective-permute-done | bytes 262176 | tf_op jit(solution)/shard_map/ppermute | solution.py:41
  256.8 10.6 %collective-permute-done.5 = bf16[1024,128]{1,0:T(8,128)(2,1)S(1)} collective-permute-done((bf16[1024,128]{1,0:T(8,128)(2,1)}, bf16[1024,128]{1,0:T(8,128)(2,1)S(1)}, u32[]{:S(2)}, u32[]{:S(2)}) %collective-permute-start.5) | collective-permute-done | bytes 262176 | tf_op jit(solution)/shard_map/ppermute | solution.py:41
  280.3 198.3 %while.52 = (s32[]{:T(128)}, bf16[8,128,4,128]{1,3,2,0:T(8,128)(2,1)}, s32[8]{0:T(128)S(1)}, bf16[4096,1,128]{2,0,1:T(8,128)(2,1)}, s32[4096]{0:T(1024)S(1)}, /*...) while((s32[]{:T(128)}, ...), condition=%wide.region_16.17_spmd, body=%wide.region_12.16_spmd.sunk | while | flops 1702372736 | bytes 31474184 | solution.py:282
  290.6 7.1 %fusion.182 = (f32[4,128]{1,0:T(4,128)S(1)}, f32[3200,128,4]{1,0,2:T(8,128)}) fusion(f32[4,128,3200]{1,2,0:T(8,128)} %get-tuple-element.851, f32[4,128]{1,0:T(4,128)S(1)} %get-tuple-element.852, bf16[1024,1,4,128]{0,3,2,1:T(8,128)(2,1)} %get-tuple-element.968, s32[]{:T(128)S(6)} %select_n.734, bf16[4096,1,128]{2,0,1:T(8,128)(2,1)} %get-tuple-element.967, ...), kind=kOutput, calls=%fused_computation.5.clone.1 | convolution fusion | flops 424345088 | bytes 14061576 | tf_op jit(solution)/shard_map/while/body/eval_jaxpr/qrd,kd->rqk/dot_general | solution.py:225
  297.7 7.6 %fusion.183 = bf16[8,128,4,128]{1,3,2,0:T(8,128)(2,1)} fusion(bf16[8,128,4,128]{1,3,2,0:T(8,128)(2,1)} %get-tuple-element.943, s32[]{:T(128)} %get-tuple-element.942, f32[3200,128,4]{1,0,2:T(8,128)} %get-tuple-element.853, f32[4,128]{1,0:T(4,128)S(1)} %get-tuple-element.854, f32[4,128]{1,0:T(4,128)S(1)} %get-tuple-element.852, ...), kind=kOutput, calls=%fused_computation.16.clone.1 | convolution fusion | flops 850398848 | bytes 9000960 | tf_op jit(solution)/shard_map/while/body/eval_jaxpr/rqk,kd->qrd/dot_general | solution.py:231
  322.5 7.5 %fusion.183 = bf16[8,128,4,128]{1,3,2,0:T(8,128)(2,1)} fusion(bf16[8,128,4,128]{1,3,2,0:T(8,128)(2,1)} %get-tuple-element.943, s32[]{:T(128)} %get-tuple-element.942, f32[3200,128,4]{1,0,2:T(8,128)} %get-tuple-element.853, f32[4,128]{1,0:T(4,128)S(1)} %get-tuple-element.854, f32[4,128]{1,0:T(4,128)S(1)} %get-tuple-element.852, ...), kind=kOutput, calls=%fused_computation.16.clone.1 | convolution fusion | flops 850398848 | bytes 9000960 | tf_op jit(solution)/shard_map/while/body/eval_jaxpr/rqk,kd->qrd/dot_general | solution.py:231
  347.3 7.5 %fusion.183 = bf16[8,128,4,128]{1,3,2,0:T(8,128)(2,1)} fusion(bf16[8,128,4,128]{1,3,2,0:T(8,128)(2,1)} %get-tuple-element.943, s32[]{:T(128)} %get-tuple-element.942, f32[3200,128,4]{1,0,2:T(8,128)} %get-tuple-element.853, f32[4,128]{1,0:T(4,128)S(1)} %get-tuple-element.854, f32[4,128]{1,0:T(4,128)S(1)} %get-tuple-element.852, ...), kind=kOutput, calls=%fused_computation.16.clone.1 | convolution fusion | flops 850398848 | bytes 9000960 | tf_op jit(solution)/shard_map/while/body/eval_jaxpr/rqk,kd->qrd/dot_general | solution.py:231
  372.0 7.5 %fusion.183 = bf16[8,128,4,128]{1,3,2,0:T(8,128)(2,1)} fusion(bf16[8,128,4,128]{1,3,2,0:T(8,128)(2,1)} %get-tuple-element.943, s32[]{:T(128)} %get-tuple-element.942, f32[3200,128,4]{1,0,2:T(8,128)} %get-tuple-element.853, f32[4,128]{1,0:T(4,128)S(1)} %get-tuple-element.854, f32[4,128]{1,0:T(4,128)S(1)} %get-tuple-element.852, ...), kind=kOutput, calls=%fused_computation.16.clone.1 | convolution fusion | flops 850398848 | bytes 9000960 | tf_op jit(solution)/shard_map/while/body/eval_jaxpr/rqk,kd->qrd/dot_general | solution.py:231
  396.8 7.5 %fusion.183 = bf16[8,128,4,128]{1,3,2,0:T(8,128)(2,1)} fusion(bf16[8,128,4,128]{1,3,2,0:T(8,128)(2,1)} %get-tuple-element.943, s32[]{:T(128)} %get-tuple-element.942, f32[3200,128,4]{1,0,2:T(8,128)} %get-tuple-element.853, f32[4,128]{1,0:T(4,128)S(1)} %get-tuple-element.854, f32[4,128]{1,0:T(4,128)S(1)} %get-tuple-element.852, ...), kind=kOutput, calls=%fused_computation.16.clone.1 | convolution fusion | flops 850398848 | bytes 9000960 | tf_op jit(solution)/shard_map/while/body/eval_jaxpr/rqk,kd->qrd/dot_general | solution.py:231
  421.5 7.5 %fusion.183 = bf16[8,128,4,128]{1,3,2,0:T(8,128)(2,1)} fusion(bf16[8,128,4,128]{1,3,2,0:T(8,128)(2,1)} %get-tuple-element.943, s32[]{:T(128)} %get-tuple-element.942, f32[3200,128,4]{1,0,2:T(8,128)} %get-tuple-element.853, f32[4,128]{1,0:T(4,128)S(1)} %get-tuple-element.854, f32[4,128]{1,0:T(4,128)S(1)} %get-tuple-element.852, ...), kind=kOutput, calls=%fused_computation.16.clone.1 | convolution fusion | flops 850398848 | bytes 9000960 | tf_op jit(solution)/shard_map/while/body/eval_jaxpr/rqk,kd->qrd/dot_general | solution.py:231
  439.3 6.9 %fusion.182 = (f32[4,128]{1,0:T(4,128)S(1)}, f32[3200,128,4]{1,0,2:T(8,128)}) fusion(f32[4,128,3200]{1,2,0:T(8,128)} %get-tuple-element.851, f32[4,128]{1,0:T(4,128)S(1)} %get-tuple-element.852, bf16[1024,1,4,128]{0,3,2,1:T(8,128)(2,1)} %get-tuple-element.968, s32[]{:T(128)S(6)} %select_n.734, bf16[4096,1,128]{2,0,1:T(8,128)(2,1)} %get-tuple-element.967, ...), kind=kOutput, calls=%fused_computation.5.clone.1 | convolution fusion | flops 424345088 | bytes 14061576 | tf_op jit(solution)/shard_map/while/body/eval_jaxpr/qrd,kd->rqk/dot_general | solution.py:225
  446.3 7.5 %fusion.183 = bf16[8,128,4,128]{1,3,2,0:T(8,128)(2,1)} fusion(bf16[8,128,4,128]{1,3,2,0:T(8,128)(2,1)} %get-tuple-element.943, s32[]{:T(128)} %get-tuple-element.942, f32[3200,128,4]{1,0,2:T(8,128)} %get-tuple-element.853, f32[4,128]{1,0:T(4,128)S(1)} %get-tuple-element.854, f32[4,128]{1,0:T(4,128)S(1)} %get-tuple-element.852, ...), kind=kOutput, calls=%fused_computation.16.clone.1 | convolution fusion | flops 850398848 | bytes 9000960 | tf_op jit(solution)/shard_map/while/body/eval_jaxpr/rqk,kd->qrd/dot_general | solution.py:231
  471.0 7.5 %fusion.183 = bf16[8,128,4,128]{1,3,2,0:T(8,128)(2,1)} fusion(bf16[8,128,4,128]{1,3,2,0:T(8,128)(2,1)} %get-tuple-element.943, s32[]{:T(128)} %get-tuple-element.942, f32[3200,128,4]{1,0,2:T(8,128)} %get-tuple-element.853, f32[4,128]{1,0:T(4,128)S(1)} %get-tuple-element.854, f32[4,128]{1,0:T(4,128)S(1)} %get-tuple-element.852, ...), kind=kOutput, calls=%fused_computation.16.clone.1 | convolution fusion | flops 850398848 | bytes 9000960 | tf_op jit(solution)/shard_map/while/body/eval_jaxpr/rqk,kd->qrd/dot_general | solution.py:231
  498.6 11.1 %all_gather.42 = f32[4,1,16]{2,1,0:T(1,128)S(1)} all-gather(f32[1,1,16]{2,1,0:T(1,128)S(1)} %copy-done.31), channel_id=1, replica_groups=mesh['ctx_0'=4,'ctx_1'=8,'head'=8] {'ctx_0'}, dimensions={0}, use_global_device_ids=true | all-gather | bytes 320 | tf_op jit(solution)/shard_map/all_gather | solution.py:28
  514.9 7.5 %multiply_reduce_fusion = bf16[4,256,256]{2,1,0:T(8,128)(2,1)S(1)} fusion(f32[4,16,256]{2,1,0:T(8,128)S(1)} %copy-done.23, pred[4,256,256]{2,1,0:T(8,128)(4,1)} %compare_and_fusion.1, bf16[4,256,16,64]{1,0,3,2:T(4,128)(2,1)} %reshape.901, bf16[4,256,16,64]{1,0,3,2:T(4,128)(2,1)} %reshape.898), kind=kOutput, calls=%fused_computation.56 | convolution fusion | flops 553385984 | bytes 5046272 | tf_op jit(solution)/shard_map/ktghp,ksghp->kghts/dot_general | solution.py:91
  538.1 8.7 %all-to-all-start.7 = ((bf16[8,128,128]{2,1,0:T(8,128)(2,1)}), bf16[8,128,128]{2,1,0:T(8,128)(2,1)S(1)}, u32[]{:S(2)}, u32[]{:S(2)}) async-start(bf16[8,128,128]{2,1,0:T(8,128)(2,1)} %bitcast.99), calls=%async_computation.7 | async-start | bytes 524288 | tf_op jit(solution)/shard_map/all_to_all | solution.py:354
  558.0 10.0 %fusion.73 = bf16[4,256,1,16,64]{1,4,3,0,2:T(8,128)(2,1)S(1)} fusion(f32[4,16,64,256]{3,2,1,0:T(8,128)} %fusion.134, f32[4,256,1,16,64]{1,0,4,3,2:T(4,128)} %reshape.908, f32[4,16,256]{2,1,0:T(8,128)S(1)} %copy-done.24, f32[4,256,256]{2,1,0:T(8,128)} %fusion.148, pred[4,256,256]{2,1,0:T(8,128)(4,1)S(1)} %copy-done.20, f32[16]{0:T(128)S(1)} %copy-done.34, ...), kind=kOutput, calls=%fused_computation.68 | convolution fusion | flops 558891008 | bytes 14024768 | tf_op jit(solution)/shard_map/kghts,ktghp->ksghp/dot_general | solution.py:88
  586.1 21.0 %all-to-all-done.5 = bf16[8,128,1024]{1,2,0:T(8,128)(2,1)S(1)} async-done(((bf16[8,128,1024]{1,2,0:T(8,128)(2,1)}), bf16[8,128,1024]{1,2,0:T(8,128)(2,1)S(1)}, u32[]{:S(2)}, u32[]{:S(2)}) %all-to-all-start.5) | async-done | bytes 2097184 | tf_op jit(solution)/shard_map/all_to_all | solution.py:352
  (325 shorter events, 367.0 us)
Async XLA Ops:
  8.7 14.2 %all-to-all-start.2 = ((bf16[128,8,16]{0,2,1:T(8,128)(2,1)}), bf16[128,8,16]{0,2,1:T(8,128)(2,1)S(1)}, u32[]{:S(2)}, u32[]{:S(2)}) async-start(bf16[128,8,16]{0,2,1:T(8,128)(2,1)} %bitcast.17), calls=%async_computation.2 | async-start | bytes 65536 | tf_op jit(solution)/shard_map/all_to_all | solution.py:327
  22.9 31.3 %all-to-all-start.4 = ((bf16[128,8,1024]{0,2,1:T(8,128)(2,1)}), bf16[128,8,1024]{0,2,1:T(8,128)(2,1)S(1)}, u32[]{:S(2)}, u32[]{:S(2)}) async-start(bf16[128,8,1024]{0,2,1:T(8,128)(2,1)} %bitcast.540), calls=%async_computation.4 | async-start | bytes 4194304 | tf_op jit(solution)/shard_map/all_to_all | solution.py:324
  31.2 23.0 %copy-start.18 = (f32[4,16,2,128]{3,2,1,0:T(2,128)}, f32[4,16,2,128]{3,2,1,0:T(2,128)S(1)}, u32[]{:S(2)}) copy-start(f32[4,16,2,128]{3,2,1,0:T(2,128)S(1)} %broadcast.608) | copy-start | bytes 196612
  54.2 13.9 %all-to-all-start.1 = ((bf16[128,8,128]{2,0,1:T(8,128)(2,1)}), bf16[128,8,128]{2,0,1:T(8,128)(2,1)S(1)}, u32[]{:S(2)}, u32[]{:S(2)}) async-start(bf16[128,8,128]{2,0,1:T(8,128)(2,1)} %copy_bitcast_fusion.4), calls=%async_computation.1 | async-start | bytes 524288 | tf_op jit(solution)/shard_map/all_to_all | solution.py:325
  58.4 95.8 %all-gather.15.cloned.1.call-start = ((), (), s32[]{:S(2)}) async-start(), calls=%async_computation.16 | async-start | bytes 4718592 | tf_op jit(solution)/shard_map/all_gather | solution.py:28
  80.5 31.3 %all-to-all-start.3 = ((bf16[128,8,1024]{0,2,1:T(8,128)(2,1)}), bf16[128,8,1024]{0,2,1:T(8,128)(2,1)S(1)}, u32[]{:S(2)}, u32[]{:S(2)}) async-start(bf16[128,8,1024]{0,2,1:T(8,128)(2,1)} %bitcast.542), calls=%async_computation.3 | async-start | bytes 4194304 | tf_op jit(solution)/shard_map/all_to_all | solution.py:328
  111.8 13.9 %all-to-all-start = ((bf16[128,8,128]{2,0,1:T(8,128)(2,1)}), bf16[128,8,128]{2,0,1:T(8,128)(2,1)S(1)}, u32[]{:S(2)}, u32[]{:S(2)}) async-start(bf16[128,8,128]{2,0,1:T(8,128)(2,1)} %copy_bitcast_fusion.5), calls=%async_computation | async-start | bytes 524288 | tf_op jit(solution)/shard_map/all_to_all | solution.py:326
  116.0 160.7 %all-gather.13.cloned.1.call-start = ((), (), s32[]{:S(2)}) async-start(), calls=%async_computation.15 | async-start | bytes 4718592 | tf_op jit(solution)/shard_map/all_gather | solution.py:28
  138.4 384.1 %all-gather.11.cloned.1.call-start = ((), (), s32[]{:S(2)}) async-start(), calls=%async_computation.14 | async-start | bytes 2621440 | tf_op jit(solution)/shard_map/all_gather | solution.py:28
  159.4 15.2 %all-to-all-start.8 = ((bf16[128,8,128]{2,0,1:T(8,128)(2,1)}), bf16[128,8,128]{2,0,1:T(8,128)(2,1)}, u32[]{:S(2)}, u32[]{:S(2)}) async-start(bf16[128,8,128]{2,0,1:T(8,128)(2,1)} %copy_bitcast_fusion.3), calls=%async_computation.8 | async-start | bytes 524288 | tf_op jit(solution)/shard_map/all_to_all | solution.py:330
  174.6 11.8 %all-to-all-start.10 = ((bf16[128,8,128]{2,0,1:T(8,128)(2,1)}), bf16[128,8,128]{2,0,1:T(8,128)(2,1)}, u32[]{:S(2)}, u32[]{:S(2)}) async-start(bf16[128,8,128]{2,0,1:T(8,128)(2,1)} %copy_bitcast_fusion.2), calls=%async_computation.10 | async-start | bytes 524288 | tf_op jit(solution)/shard_map/all_to_all | solution.py:331
  186.4 31.5 %all-to-all-start.9 = ((bf16[128,8,512]{0,2,1:T(8,128)(2,1)}), bf16[128,8,512]{0,2,1:T(8,128)(2,1)S(1)}, u32[]{:S(2)}, u32[]{:S(2)}) async-start(bf16[128,8,512]{0,2,1:T(8,128)(2,1)} %bitcast.548), calls=%async_computation.9 | async-start | bytes 2097152 | tf_op jit(solution)/shard_map/all_to_all | solution.py:329
  197.4 26.8 %collective-permute-start = (bf16[1024,128]{1,0:T(8,128)(2,1)}, bf16[1024,128]{1,0:T(8,128)(2,1)}, u32[]{:S(2)}, u32[]{:S(2)}) collective-permute-start(bf16[1024,128]{1,0:T(8,128)(2,1)} %bitcast.102), channel_id=1, source_target_pairs={{0,24},{8,32},{16,40},{24,48},{32,56},{40,64},{48,72},{56,80},{64,... | collective-permute-start | bytes 786440 | tf_op jit(solution)/shard_map/ppermute | solution.py:41
  200.3 27.0 %collective-permute-start.1 = (bf16[1024,128]{1,0:T(8,128)(2,1)}, bf16[1024,128]{1,0:T(8,128)(2,1)}, u32[]{:S(2)}, u32[]{:S(2)}) collective-permute-start(bf16[1024,128]{1,0:T(8,128)(2,1)} %bitcast.102), channel_id=1, source_target_pairs={{0,16},{8,24},{16,32},{24,40},{32,48},{40,56},{48,64},{56,72},{64,... | collective-permute-start | bytes 786440 | tf_op jit(solution)/shard_map/ppermute | solution.py:41
  205.4 28.3 %collective-permute-start.2 = (bf16[1024,128]{1,0:T(8,128)(2,1)}, bf16[1024,128]{1,0:T(8,128)(2,1)}, u32[]{:S(2)}, u32[]{:S(2)}) collective-permute-start(bf16[1024,128]{1,0:T(8,128)(2,1)} %bitcast.102), channel_id=1, source_target_pairs={{0,8},{8,16},{16,24},{24,32},{32,40},{40,48},{48,56},{56,64},{64,7... | collective-permute-start | bytes 786440 | tf_op jit(solution)/shard_map/ppermute | solution.py:41
  207.4 41.8 %collective-permute-start.3 = (bf16[1024,128]{1,0:T(8,128)(2,1)}, bf16[1024,128]{1,0:T(8,128)(2,1)}, u32[]{:S(2)}, u32[]{:S(2)}) collective-permute-start(bf16[1024,128]{1,0:T(8,128)(2,1)} %bitcast.108), channel_id=1, source_target_pairs={{0,24},{8,32},{16,40},{24,48},{32,56},{40,64},{48,72},{56,80},{64,... | collective-permute-start | bytes 786440 | tf_op jit(solution)/shard_map/ppermute | solution.py:41
  212.4 44.4 %collective-permute-start.4 = (bf16[1024,128]{1,0:T(8,128)(2,1)}, bf16[1024,128]{1,0:T(8,128)(2,1)}, u32[]{:S(2)}, u32[]{:S(2)}) collective-permute-start(bf16[1024,128]{1,0:T(8,128)(2,1)} %bitcast.108), channel_id=1, source_target_pairs={{0,16},{8,24},{16,32},{24,40},{32,48},{40,56},{48,64},{56,72},{64,... | collective-permute-start | bytes 786440 | tf_op jit(solution)/shard_map/ppermute | solution.py:41
  217.9 55.6 %all-to-all-start.11 = ((bf16[128,8,512]{0,2,1:T(8,128)(2,1)}), bf16[128,8,512]{0,2,1:T(8,128)(2,1)}, u32[]{:S(2)}, u32[]{:S(2)}) async-start(bf16[128,8,512]{0,2,1:T(8,128)(2,1)} %bitcast.111), calls=%async_computation.11 | async-start | bytes 2097152 | tf_op jit(solution)/shard_map/all_to_all | solution.py:332
  224.1 304.3 %all-gather.9.cloned.1.call-start = ((), (), s32[]{:S(2)}) async-start(), calls=%async_computation.13 | async-start | bytes 2621440 | tf_op jit(solution)/shard_map/all_gather | solution.py:28
  224.1 43.3 %collective-permute-start.5 = (bf16[1024,128]{1,0:T(8,128)(2,1)}, bf16[1024,128]{1,0:T(8,128)(2,1)S(1)}, u32[]{:S(2)}, u32[]{:S(2)}) collective-permute-start(bf16[1024,128]{1,0:T(8,128)(2,1)} %bitcast.108), channel_id=1, source_target_pairs={{0,8},{8,16},{16,24},{24,32},{32,40},{40,48},{48,56},{56,64},{64,7... | collective-permute-start | bytes 786440 | tf_op jit(solution)/shard_map/ppermute | solution.py:41
  480.8 57.3 %all-to-all-start.12 = ((bf16[8,128,512]{2,1,0:T(8,128)(2,1)}), bf16[8,128,512]{2,1,0:T(8,128)(2,1)}, u32[]{:S(2)}, u32[]{:S(2)}) async-start(bf16[8,128,512]{2,1,0:T(8,128)(2,1)} %copy.289), calls=%async_computation.12 | async-start | bytes 2097152 | tf_op jit(solution)/shard_map/all_to_all | solution.py:355
  538.1 15.2 %all-to-all-start.7 = ((bf16[8,128,128]{2,1,0:T(8,128)(2,1)}), bf16[8,128,128]{2,1,0:T(8,128)(2,1)S(1)}, u32[]{:S(2)}, u32[]{:S(2)}) async-start(bf16[8,128,128]{2,1,0:T(8,128)(2,1)} %bitcast.99), calls=%async_computation.7 | async-start | bytes 524288 | tf_op jit(solution)/shard_map/all_to_all | solution.py:354
  553.3 21.9 %all-to-all-start.6 = ((bf16[8,128,128]{2,1,0:T(8,128)(2,1)}), bf16[8,128,128]{2,1,0:T(8,128)(2,1)S(1)}, u32[]{:S(2)}, u32[]{:S(2)}) async-start(bf16[8,128,128]{2,1,0:T(8,128)(2,1)} %bitcast.78), calls=%async_computation.6 | async-start | bytes 524288 | tf_op jit(solution)/shard_map/all_to_all | solution.py:353
  575.9 31.2 %all-to-all-start.5 = ((bf16[8,128,1024]{1,2,0:T(8,128)(2,1)}), bf16[8,128,1024]{1,2,0:T(8,128)(2,1)S(1)}, u32[]{:S(2)}, u32[]{:S(2)}) async-start(bf16[8,128,1024]{1,2,0:T(8,128)(2,1)} %copy.256), calls=%async_computation.5 | async-start | bytes 4194304 | tf_op jit(solution)/shard_map/all_to_all | solution.py:352
  (34 other events, 305.6 us)
Sparse Core Ops, SparseCore 0:
  76.5 56.9 all-gather.14
  138.5 56.9 all-gather.12
  197.3 44.2 all-gather.10
  280.4 34.4 all-gather.8
where the time goes:
time: 628 us; the launch traced here: 617 us
  matrix products  196 us (31%)
  waiting for transfers between devices  118 us (19%)
  starting transfers between devices  94.8 us (15%)
  local copies, waits for them, and re-layouts  84.4 us (13%)
  other arithmetic  72.5 us (12%)
  blocking collectives  30.8 us (5%)
  between operations  14.9 us (2%)
    dot_general x8, matrix products, attend_block(): jnp.einsum('rqk,kd->qrd', grad_logits, key_block, preferred_element_type=...  60 us
    dot_general x8, matrix products, attend_block(): jnp.einsum('qrd,kd->rqk', grad_block, value_block, preferred_element_type...  55.8 us
    sub x8, matrix products, attend_block(): weights = jnp.exp(logits - row_peaks)  47.3 us
    ppermute x6, waiting for transfers between devices, from_behind(): lax.ppermute(value, axis, [(source, source + steps) for source in range(l...  37.8 us
    all_gather x3, blocking collectives, entering_2(): pieces = jax.tree.map(lambda part: lax.all_gather(part, axis), so_far)  30.8 us
    all_to_all x1, waiting for transfers between devices, shards(): lax.all_to_all(mixer_grad, 'head', split_axis=1, concat_axis=0, tiled=True)  25.5 us
    and x8, other arithmetic, attend_block(): (key_pos[None, :] <= query_pos[:, None]) & (key_pos[None, :] >= 0)  22.5 us
    all_to_all x1, waiting for transfers between devices, shards(): lax.all_to_all(mixer_input, 'head', split_axis=1, concat_axis=0, tiled=True)  22.2 us
  transfers between devices with their start and end apart: 23, of which 10 were waited for; matrix products, arithmetic and copies ran while one was open for 55% of the time, Pallas kernels for 0%

commit v1 on v0

--- a/solution.py
+++ b/solution.py
@@ -351,7 +351,12 @@
     returned = (
         lax.all_to_all(grad_input, "head", split_axis=0, concat_axis=1, tiled=True),
         lax.all_to_all(grad_write, "head", split_axis=0, concat_axis=1, tiled=True),
-        lax.all_to_all(grad_read, "head", split_axis=0, concat_axis=1, tiled=True),
+        jnp.concatenate(
+            lax.all_to_all(
+                jnp.stack(jnp.split(grad_read, lax.axis_size("head"), axis=0)), "head", 0, 0
+            ),
+            axis=1,
+        ),
         lax.all_to_all(grad_query_heads, "head", split_axis=0, concat_axis=1, tiled=True),
     )
     return (returned[0], returned[1], returned[2], returned[3])

time: 628 us -> 657 us (1.046)
  waiting for transfers between devices: 118 us -> 151 us
    all_gather x4, waiting for transfers between devices: 0.03 us -> 17 us  [entering_2(): pieces = jax.tree.map(lambda part: lax.all_gather(part, axis), so_far)]
    ppermute x6, waiting for transfers between devices: 37.8 us -> 54.4 us  [from_behind(): lax.ppermute(value, axis, [(source, source + steps) for source in range(l...]
    unnamed x78 -> x75, local copies, waits for them, and re-layouts: 19.9 us -> 25.2 us
  transfers between devices with their start and end apart: 23 -> 23, of which waited for: 10 -> 12; matrix products, arithmetic and copies ran while one was open for 55% -> 52% of each run, Pallas kernels for 0% -> 0%
where the time goes in v1:
time: 657 us; the launch traced here: 646 us
  matrix products  194 us (30%)
  waiting for transfers between devices  151 us (23%)
  starting transfers between devices  94.9 us (14%)
  local copies, waits for them, and re-layouts  90.2 us (14%)
  other arithmetic  68.8 us (10%)
  blocking collectives  26.4 us (4%)
  between operations  14.8 us (2%)
    dot_general x8, matrix products, attend_block(): jnp.einsum('rqk,kd->qrd', grad_logits, key_block, preferred_element_type=...  60 us
    dot_general x8, matrix products, attend_block(): jnp.einsum('qrd,kd->rqk', grad_block, value_block, preferred_element_type...  55.6 us
    ppermute x6, waiting for transfers between devices, from_behind(): lax.ppermute(value, axis, [(source, source + steps) for source in range(l...  54.4 us
    sub x8, matrix products, attend_block(): weights = jnp.exp(logits - row_peaks)  47.1 us
    all_gather x3, blocking collectives, entering_2(): pieces = jax.tree.map(lambda part: lax.all_gather(part, axis), so_far)  26.4 us
    ppermute x6, starting transfers between devices, from_behind(): lax.ppermute(value, axis, [(source, source + steps) for source in range(l...  25.7 us
    all_to_all x1, waiting for transfers between devices, shards(): lax.all_to_all(mixer_grad, 'head', split_axis=1, concat_axis=0, tiled=True)  25.5 us
    unnamed x75, local copies, waits for them, and re-layouts  25.2 us
  transfers between devices with their start and end apart: 23, of which 12 were waited for; matrix products, arithmetic and copies ran while one was open for 52% of the time, Pallas kernels for 0%

profile of v1, /device:TPU:1, one launch (start us, length us, event | category | flops | bytes accessed | tf_op | source)
XLA Modules:
  0.0 645.7 jit_solution(9055941103544988271)
XLA Ops:
  32.0 22.2 %all-to-all-done.4 = bf16[128,8,1024]{0,2,1:T(8,128)(2,1)S(1)} async-done(((bf16[128,8,1024]{0,2,1:T(8,128)(2,1)}), bf16[128,8,1024]{0,2,1:T(8,128)(2,1)S(1)}, u32[]{:S(2)}, u32[]{:S(2)}) %all-to-all-start.4) | async-done | bytes 2097184 | tf_op jit(solution)/shard_map/all_to_all | solution.py:324
  86.2 25.5 %all-to-all-done.3 = bf16[128,8,1024]{0,2,1:T(8,128)(2,1)S(1)} async-done(((bf16[128,8,1024]{0,2,1:T(8,128)(2,1)}), bf16[128,8,1024]{0,2,1:T(8,128)(2,1)S(1)}, u32[]{:S(2)}, u32[]{:S(2)}) %all-to-all-start.3) | async-done | bytes 2097184 | tf_op jit(solution)/shard_map/all_to_all | solution.py:328
  129.4 8.2 %while.53 = (s32[]{:T(128)}, f32[1,16,64,128]{3,2,1,0:T(8,128)S(1)}, f32[1,16]{1,0:T(1,128)S(1)}, f32[4,1,16,64,128]{4,3,2,1,0:T(8,128)}, f32[4,1,16]{2,1,0:T(1,...) while((s32[]{:T(128)}, ...), condition=%wide.region_7.8_spmd.clone, body=%wide.region_6.7_spmd.clone.sunk | while | flops 524340 | bytes 2622994 | solution.py:176
  202.8 10.3 %collective-permute-done.1 = bf16[1024,128]{1,0:T(8,128)(2,1)} collective-permute-done((bf16[1024,128]{1,0:T(8,128)(2,1)S(1)}, bf16[1024,128]{1,0:T(8,128)(2,1)}, u32[]{:S(2)}, u32[]{:S(2)}) %collective-permute-start.1) | collective-permute-done | bytes 262176 | tf_op jit(solution)/shard_map/ppermute | solution.py:41
  213.0 12.5 %collective-permute-done.2 = bf16[1024,128]{1,0:T(8,128)(2,1)} collective-permute-done((bf16[1024,128]{1,0:T(8,128)(2,1)S(1)}, bf16[1024,128]{1,0:T(8,128)(2,1)}, u32[]{:S(2)}, u32[]{:S(2)}) %collective-permute-start.2) | collective-permute-done | bytes 262176 | tf_op jit(solution)/shard_map/ppermute | solution.py:41
  227.7 13.4 %collective-permute-done.3 = bf16[1024,128]{1,0:T(8,128)(2,1)S(1)} collective-permute-done((bf16[1024,128]{1,0:T(8,128)(2,1)S(1)}, bf16[1024,128]{1,0:T(8,128)(2,1)S(1)}, u32[]{:S(2)}, u32[]{:S(2)}) %collective-permute-start.3) | collective-permute-done | bytes 262176 | tf_op jit(solution)/shard_map/ppermute | solution.py:41
  241.2 9.6 %collective-permute-done.4 = bf16[1024,128]{1,0:T(8,128)(2,1)} collective-permute-done((bf16[1024,128]{1,0:T(8,128)(2,1)S(1)}, bf16[1024,128]{1,0:T(8,128)(2,1)}, u32[]{:S(2)}, u32[]{:S(2)}) %collective-permute-start.4) | collective-permute-done | bytes 262176 | tf_op jit(solution)/shard_map/ppermute | solution.py:41
  250.8 8.6 %collective-permute-done.5 = bf16[1024,128]{1,0:T(8,128)(2,1)S(1)} collective-permute-done((bf16[1024,128]{1,0:T(8,128)(2,1)S(1)}, bf16[1024,128]{1,0:T(8,128)(2,1)S(1)}, u32[]{:S(2)}, u32[]{:S(2)}) %collective-permute-start.5) | collective-permute-done | bytes 262176 | tf_op jit(solution)/shard_map/ppermute | solution.py:41
  271.8 13.8 %all-gather.3 = f32[8,1,16]{2,1,0:T(1,128)S(1)} all-gather(f32[1,1,16]{2,1,0:T(1,128)S(1)} %bitcast.610), channel_id=2, replica_groups=mesh['ctx_0'=4,'ctx_1'=8,'head'=8] {'ctx_1'}, dimensions={0}, use_global_device_ids=true | all-gather | bytes 576 | tf_op jit(solution)/shard_map/all_gather | solution.py:28
  289.1 197.8 %while.52 = (s32[]{:T(128)}, bf16[8,128,4,128]{1,3,2,0:T(8,128)(2,1)}, s32[8]{0:T(128)S(1)}, bf16[4096,1,128]{2,0,1:T(8,128)(2,1)}, s32[4096]{0:T(1024)S(1)}, /*...) while((s32[]{:T(128)}, ...), condition=%wide.region_16.17_spmd, body=%wide.region_12.16_spmd.sunk | while | flops 1702372736 | bytes 31474184 | solution.py:282
  306.4 7.5 %fusion.191 = bf16[8,128,4,128]{1,3,2,0:T(8,128)(2,1)} fusion(bf16[8,128,4,128]{1,3,2,0:T(8,128)(2,1)} %get-tuple-element.943, s32[]{:T(128)} %get-tuple-element.942, f32[3200,128,4]{1,0,2:T(8,128)} %get-tuple-element.853, f32[4,128]{1,0:T(4,128)S(1)} %get-tuple-element.854, f32[4,128]{1,0:T(4,128)S(1)} %get-tuple-element.852, ...), kind=kOutput, calls=%fused_computation.16.clone.1 | convolution fusion | flops 850398848 | bytes 9000960 | tf_op jit(solution)/shard_map/while/body/eval_jaxpr/rqk,kd->qrd/dot_general | solution.py:231
  331.1 7.5 %fusion.191 = bf16[8,128,4,128]{1,3,2,0:T(8,128)(2,1)} fusion(bf16[8,128,4,128]{1,3,2,0:T(8,128)(2,1)} %get-tuple-element.943, s32[]{:T(128)} %get-tuple-element.942, f32[3200,128,4]{1,0,2:T(8,128)} %get-tuple-element.853, f32[4,128]{1,0:T(4,128)S(1)} %get-tuple-element.854, f32[4,128]{1,0:T(4,128)S(1)} %get-tuple-element.852, ...), kind=kOutput, calls=%fused_computation.16.clone.1 | convolution fusion | flops 850398848 | bytes 9000960 | tf_op jit(solution)/shard_map/while/body/eval_jaxpr/rqk,kd->qrd/dot_general | solution.py:231
  355.8 7.5 %fusion.191 = bf16[8,128,4,128]{1,3,2,0:T(8,128)(2,1)} fusion(bf16[8,128,4,128]{1,3,2,0:T(8,128)(2,1)} %get-tuple-element.943, s32[]{:T(128)} %get-tuple-element.942, f32[3200,128,4]{1,0,2:T(8,128)} %get-tuple-element.853, f32[4,128]{1,0:T(4,128)S(1)} %get-tuple-element.854, f32[4,128]{1,0:T(4,128)S(1)} %get-tuple-element.852, ...), kind=kOutput, calls=%fused_computation.16.clone.1 | convolution fusion | flops 850398848 | bytes 9000960 | tf_op jit(solution)/shard_map/while/body/eval_jaxpr/rqk,kd->qrd/dot_general | solution.py:231
  380.5 7.5 %fusion.191 = bf16[8,128,4,128]{1,3,2,0:T(8,128)(2,1)} fusion(bf16[8,128,4,128]{1,3,2,0:T(8,128)(2,1)} %get-tuple-element.943, s32[]{:T(128)} %get-tuple-element.942, f32[3200,128,4]{1,0,2:T(8,128)} %get-tuple-element.853, f32[4,128]{1,0:T(4,128)S(1)} %get-tuple-element.854, f32[4,128]{1,0:T(4,128)S(1)} %get-tuple-element.852, ...), kind=kOutput, calls=%fused_computation.16.clone.1 | convolution fusion | flops 850398848 | bytes 9000960 | tf_op jit(solution)/shard_map/while/body/eval_jaxpr/rqk,kd->qrd/dot_general | solution.py:231
  405.3 7.5 %fusion.191 = bf16[8,128,4,128]{1,3,2,0:T(8,128)(2,1)} fusion(bf16[8,128,4,128]{1,3,2,0:T(8,128)(2,1)} %get-tuple-element.943, s32[]{:T(128)} %get-tuple-element.942, f32[3200,128,4]{1,0,2:T(8,128)} %get-tuple-element.853, f32[4,128]{1,0:T(4,128)S(1)} %get-tuple-element.854, f32[4,128]{1,0:T(4,128)S(1)} %get-tuple-element.852, ...), kind=kOutput, calls=%fused_computation.16.clone.1 | convolution fusion | flops 850398848 | bytes 9000960 | tf_op jit(solution)/shard_map/while/body/eval_jaxpr/rqk,kd->qrd/dot_general | solution.py:231
  430.0 7.5 %fusion.191 = bf16[8,128,4,128]{1,3,2,0:T(8,128)(2,1)} fusion(bf16[8,128,4,128]{1,3,2,0:T(8,128)(2,1)} %get-tuple-element.943, s32[]{:T(128)} %get-tuple-element.942, f32[3200,128,4]{1,0,2:T(8,128)} %get-tuple-element.853, f32[4,128]{1,0:T(4,128)S(1)} %get-tuple-element.854, f32[4,128]{1,0:T(4,128)S(1)} %get-tuple-element.852, ...), kind=kOutput, calls=%fused_computation.16.clone.1 | convolution fusion | flops 850398848 | bytes 9000960 | tf_op jit(solution)/shard_map/while/body/eval_jaxpr/rqk,kd->qrd/dot_general | solution.py:231
  454.7 7.5 %fusion.191 = bf16[8,128,4,128]{1,3,2,0:T(8,128)(2,1)} fusion(bf16[8,128,4,128]{1,3,2,0:T(8,128)(2,1)} %get-tuple-element.943, s32[]{:T(128)} %get-tuple-element.942, f32[3200,128,4]{1,0,2:T(8,128)} %get-tuple-element.853, f32[4,128]{1,0:T(4,128)S(1)} %get-tuple-element.854, f32[4,128]{1,0:T(4,128)S(1)} %get-tuple-element.852, ...), kind=kOutput, calls=%fused_computation.16.clone.1 | convolution fusion | flops 850398848 | bytes 9000960 | tf_op jit(solution)/shard_map/while/body/eval_jaxpr/rqk,kd->qrd/dot_general | solution.py:231
  479.4 7.5 %fusion.191 = bf16[8,128,4,128]{1,3,2,0:T(8,128)(2,1)} fusion(bf16[8,128,4,128]{1,3,2,0:T(8,128)(2,1)} %get-tuple-element.943, s32[]{:T(128)} %get-tuple-element.942, f32[3200,128,4]{1,0,2:T(8,128)} %get-tuple-element.853, f32[4,128]{1,0:T(4,128)S(1)} %get-tuple-element.854, f32[4,128]{1,0:T(4,128)S(1)} %get-tuple-element.852, ...), kind=kOutput, calls=%fused_computation.16.clone.1 | convolution fusion | flops 850398848 | bytes 9000960 | tf_op jit(solution)/shard_map/while/body/eval_jaxpr/rqk,kd->qrd/dot_general | solution.py:231
  489.2 8.9 %all-to-all-start.12 = ((bf16[8,128,512]{2,1,0:T(8,128)(2,1)}), bf16[8,128,512]{2,1,0:T(8,128)(2,1)}, u32[]{:S(2)}, u32[]{:S(2)}) async-start(bf16[8,128,512]{2,1,0:T(8,128)(2,1)} %copy.289), calls=%async_computation.12 | async-start | bytes 2097152 | tf_op jit(solution)/shard_map/all_to_all | solution.py:360
  510.3 7.2 %all_gather.42 = f32[4,1,16]{2,1,0:T(1,128)S(1)} all-gather(f32[1,1,16]{2,1,0:T(1,128)S(1)} %get-tuple-element.685), channel_id=1, replica_groups=mesh['ctx_0'=4,'ctx_1'=8,'head'=8] {'ctx_0'}, dimensions={0}, use_global_device_ids=true | all-gather | bytes 320 | tf_op jit(solution)/shard_map/all_gather | solution.py:28
  526.4 8.2 %multiply_reduce_fusion = bf16[4,256,256]{2,1,0:T(8,128)(2,1)} fusion(f32[4,16,256]{2,1,0:T(8,128)S(1)} %copy-done.23, pred[4,256,256]{2,1,0:T(8,128)(4,1)S(1)} %copy-done.20, bf16[4,256,16,64]{1,0,3,2:T(4,128)(2,1)} %reshape.905, bf16[4,256,16,64]{1,0,3,2:T(4,128)(2,1)} %reshape.902), kind=kOutput, calls=%fused_computation.56 | convolution fusion | flops 553385984 | bytes 5046272 | tf_op jit(solution)/shard_map/ktghp,ksghp->kghts/dot_general | solution.py:91
  544.4 16.9 %all-gather.9.cloned.1.call-done = f32[4,1,16,64,128]{4,3,2,1,0:T(8,128)} async-done(((f32[1,1,16,64,128]{4,3,2,1,0:T(8,128)}), f32[4,1,16,64,128]{4,3,2,1,0:T(8,128)}) %all-gather.9.cloned.1.call-update) | async-done | bytes 2097168 | tf_op jit(solution)/shard_map/all_gather | solution.py:28
  586.8 10.0 %fusion.73 = bf16[4,256,1,16,64]{1,4,3,0,2:T(8,128)(2,1)S(1)} fusion(f32[4,16,64,256]{3,2,1,0:T(8,128)} %fusion.142, f32[4,256,1,16,64]{1,0,4,3,2:T(4,128)} %reshape.915, f32[4,16,256]{2,1,0:T(8,128)S(1)} %copy-done.24, f32[4,256,256]{2,1,0:T(8,128)} %fusion.156, pred[4,256,256]{2,1,0:T(8,128)(4,1)S(1)} %copy-done.20, f32[16]{0:T(128)S(1)} %copy-done.29, ...), kind=kOutput, calls=%fused_computation.68 | convolution fusion | flops 558891008 | bytes 14024768 | tf_op jit(solution)/shard_map/kghts,ktghp->ksghp/dot_general | solution.py:88
  614.9 20.9 %all-to-all-done.5 = bf16[8,128,1024]{1,2,0:T(8,128)(2,1)S(1)} async-done(((bf16[8,128,1024]{1,2,0:T(8,128)(2,1)}), bf16[8,128,1024]{1,2,0:T(8,128)(2,1)S(1)}, u32[]{:S(2)}, u32[]{:S(2)}) %all-to-all-start.5) | async-done | bytes 2097184 | tf_op jit(solution)/shard_map/all_to_all | solution.py:352
  (323 shorter events, 382.2 us)
Async XLA Ops:
  8.7 14.2 %all-to-all-start.2 = ((bf16[128,8,16]{0,2,1:T(8,128)(2,1)}), bf16[128,8,16]{0,2,1:T(8,128)(2,1)S(1)}, u32[]{:S(2)}, u32[]{:S(2)}) async-start(bf16[128,8,16]{0,2,1:T(8,128)(2,1)} %bitcast.17), calls=%async_computation.2 | async-start | bytes 65536 | tf_op jit(solution)/shard_map/all_to_all | solution.py:327
  22.9 31.3 %all-to-all-start.4 = ((bf16[128,8,1024]{0,2,1:T(8,128)(2,1)}), bf16[128,8,1024]{0,2,1:T(8,128)(2,1)S(1)}, u32[]{:S(2)}, u32[]{:S(2)}) async-start(bf16[128,8,1024]{0,2,1:T(8,128)(2,1)} %bitcast.572), calls=%async_computation.4 | async-start | bytes 4194304 | tf_op jit(solution)/shard_map/all_to_all | solution.py:324
  31.9 29.2 %copy-start.21 = (f32[4,256,1,16]{1,3,2,0:T(8,128)}, f32[4,256,1,16]{1,3,2,0:T(8,128)S(1)}, u32[]{:S(2)}) copy-start(f32[4,256,1,16]{1,3,2,0:T(8,128)S(1)} %copy.332) | copy-start | bytes 196612
  54.2 13.9 %all-to-all-start.1 = ((bf16[128,8,128]{2,0,1:T(8,128)(2,1)}), bf16[128,8,128]{2,0,1:T(8,128)(2,1)S(1)}, u32[]{:S(2)}, u32[]{:S(2)}) async-start(bf16[128,8,128]{2,0,1:T(8,128)(2,1)} %copy_bitcast_fusion.4), calls=%async_computation.1 | async-start | bytes 524288 | tf_op jit(solution)/shard_map/all_to_all | solution.py:325
  58.4 227.3 %all-gather.15.cloned.1.call-start = ((), (), s32[]{:S(2)}) async-start(), calls=%async_computation.16 | async-start | bytes 4718592 | tf_op jit(solution)/shard_map/all_gather | solution.py:28
  80.5 31.3 %all-to-all-start.3 = ((bf16[128,8,1024]{0,2,1:T(8,128)(2,1)}), bf16[128,8,1024]{0,2,1:T(8,128)(2,1)S(1)}, u32[]{:S(2)}, u32[]{:S(2)}) async-start(bf16[128,8,1024]{0,2,1:T(8,128)(2,1)} %bitcast.574), calls=%async_computation.3 | async-start | bytes 4194304 | tf_op jit(solution)/shard_map/all_to_all | solution.py:328
  111.8 13.9 %all-to-all-start = ((bf16[128,8,128]{2,0,1:T(8,128)(2,1)}), bf16[128,8,128]{2,0,1:T(8,128)(2,1)S(1)}, u32[]{:S(2)}, u32[]{:S(2)}) async-start(bf16[128,8,128]{2,0,1:T(8,128)(2,1)} %copy_bitcast_fusion.5), calls=%async_computation | async-start | bytes 524288 | tf_op jit(solution)/shard_map/all_to_all | solution.py:326
  116.0 406.9 %all-gather.13.cloned.1.call-start = ((), (), s32[]{:S(2)}) async-start(), calls=%async_computation.15 | async-start | bytes 4718592 | tf_op jit(solution)/shard_map/all_gather | solution.py:28
  140.1 11.3 %all-to-all-start.8 = ((bf16[128,8,128]{2,0,1:T(8,128)(2,1)}), bf16[128,8,128]{2,0,1:T(8,128)(2,1)S(1)}, u32[]{:S(2)}, u32[]{:S(2)}) async-start(bf16[128,8,128]{2,0,1:T(8,128)(2,1)} %copy_bitcast_fusion.3), calls=%async_computation.8 | async-start | bytes 524288 | tf_op jit(solution)/shard_map/all_to_all | solution.py:330
  151.4 10.9 %all-to-all-start.10 = ((bf16[128,8,128]{2,0,1:T(8,128)(2,1)}), bf16[128,8,128]{2,0,1:T(8,128)(2,1)S(1)}, u32[]{:S(2)}, u32[]{:S(2)}) async-start(bf16[128,8,128]{2,0,1:T(8,128)(2,1)} %copy_bitcast_fusion.2), calls=%async_computation.10 | async-start | bytes 524288 | tf_op jit(solution)/shard_map/all_to_all | solution.py:331
  162.3 29.4 %all-to-all-start.9 = ((bf16[128,8,512]{0,2,1:T(8,128)(2,1)}), bf16[128,8,512]{0,2,1:T(8,128)(2,1)}, u32[]{:S(2)}, u32[]{:S(2)}) async-start(bf16[128,8,512]{0,2,1:T(8,128)(2,1)} %bitcast.580), calls=%async_computation.9 | async-start | bytes 2097152 | tf_op jit(solution)/shard_map/all_to_all | solution.py:329
  169.6 28.4 %collective-permute-start = (bf16[1024,128]{1,0:T(8,128)(2,1)S(1)}, bf16[1024,128]{1,0:T(8,128)(2,1)}, u32[]{:S(2)}, u32[]{:S(2)}) collective-permute-start(bf16[1024,128]{1,0:T(8,128)(2,1)S(1)} %bitcast.598), channel_id=1, source_target_pairs={{0,24},{8,32},{16,40},{24,48},{32,56},{40,64},{48,72},{56,80},{64,... | collective-permute-start | bytes 786440 | tf_op jit(solution)/shard_map/ppermute | solution.py:41
  175.9 37.1 %collective-permute-start.1 = (bf16[1024,128]{1,0:T(8,128)(2,1)S(1)}, bf16[1024,128]{1,0:T(8,128)(2,1)}, u32[]{:S(2)}, u32[]{:S(2)}) collective-permute-start(bf16[1024,128]{1,0:T(8,128)(2,1)S(1)} %bitcast.599), channel_id=1, source_target_pairs={{0,16},{8,24},{16,32},{24,40},{32,48},{40,56},{48,64},{56,72},{64,... | collective-permute-start | bytes 786440 | tf_op jit(solution)/shard_map/ppermute | solution.py:41
  181.7 43.8 %collective-permute-start.2 = (bf16[1024,128]{1,0:T(8,128)(2,1)S(1)}, bf16[1024,128]{1,0:T(8,128)(2,1)}, u32[]{:S(2)}, u32[]{:S(2)}) collective-permute-start(bf16[1024,128]{1,0:T(8,128)(2,1)S(1)} %bitcast.600), channel_id=1, source_target_pairs={{0,8},{8,16},{16,24},{24,32},{32,40},{40,48},{48,56},{56,64},{64,7... | collective-permute-start | bytes 786440 | tf_op jit(solution)/shard_map/ppermute | solution.py:41
  184.4 56.8 %collective-permute-start.3 = (bf16[1024,128]{1,0:T(8,128)(2,1)S(1)}, bf16[1024,128]{1,0:T(8,128)(2,1)S(1)}, u32[]{:S(2)}, u32[]{:S(2)}) collective-permute-start(bf16[1024,128]{1,0:T(8,128)(2,1)S(1)} %bitcast.594), channel_id=1, source_target_pairs={{0,24},{8,32},{16,40},{24,48},{32,56},{40,64},{48,72},{56,80},{64,... | collective-permute-start | bytes 786440 | tf_op jit(solution)/shard_map/ppermute | solution.py:41
  185.7 65.0 %collective-permute-start.4 = (bf16[1024,128]{1,0:T(8,128)(2,1)S(1)}, bf16[1024,128]{1,0:T(8,128)(2,1)}, u32[]{:S(2)}, u32[]{:S(2)}) collective-permute-start(bf16[1024,128]{1,0:T(8,128)(2,1)S(1)} %bitcast.595), channel_id=1, source_target_pairs={{0,16},{8,24},{16,32},{24,40},{32,48},{40,56},{48,64},{56,72},{64,... | collective-permute-start | bytes 786440 | tf_op jit(solution)/shard_map/ppermute | solution.py:41
  191.7 74.9 %all-to-all-start.11 = ((bf16[128,8,512]{0,2,1:T(8,128)(2,1)}), bf16[128,8,512]{0,2,1:T(8,128)(2,1)}, u32[]{:S(2)}, u32[]{:S(2)}) async-start(bf16[128,8,512]{0,2,1:T(8,128)(2,1)} %bitcast.579), calls=%async_computation.11 | async-start | bytes 2097152 | tf_op jit(solution)/shard_map/all_to_all | solution.py:332
  198.0 336.7 %all-gather.11.cloned.1.call-start = ((), (), s32[]{:S(2)}) async-start(), calls=%async_computation.14 | async-start | bytes 2621440 | tf_op jit(solution)/shard_map/all_gather | solution.py:28
  198.0 61.4 %collective-permute-start.5 = (bf16[1024,128]{1,0:T(8,128)(2,1)S(1)}, bf16[1024,128]{1,0:T(8,128)(2,1)S(1)}, u32[]{:S(2)}, u32[]{:S(2)}) collective-permute-start(bf16[1024,128]{1,0:T(8,128)(2,1)S(1)} %bitcast.596), channel_id=1, source_target_pairs={{0,8},{8,16},{16,24},{24,32},{32,40},{40,48},{48,56},{56,64},{64,7... | collective-permute-start | bytes 786440 | tf_op jit(solution)/shard_map/ppermute | solution.py:41
  489.2 81.3 %all-to-all-start.12 = ((bf16[8,128,512]{2,1,0:T(8,128)(2,1)}), bf16[8,128,512]{2,1,0:T(8,128)(2,1)}, u32[]{:S(2)}, u32[]{:S(2)}) async-start(bf16[8,128,512]{2,1,0:T(8,128)(2,1)} %copy.289), calls=%async_computation.12 | async-start | bytes 2097152 | tf_op jit(solution)/shard_map/all_to_all | solution.py:360
  498.1 63.2 %all-gather.9.cloned.1.call-start = ((), (), s32[]{:S(2)}) async-start(), calls=%async_computation.13 | async-start | bytes 2621440 | tf_op jit(solution)/shard_map/all_gather | solution.py:28
  570.5 11.6 %all-to-all-start.7 = ((bf16[8,128,128]{2,1,0:T(8,128)(2,1)}), bf16[8,128,128]{2,1,0:T(8,128)(2,1)S(1)}, u32[]{:S(2)}, u32[]{:S(2)}) async-start(bf16[8,128,128]{2,1,0:T(8,128)(2,1)} %fusion.132), calls=%async_computation.7 | async-start | bytes 524288 | tf_op jit(solution)/shard_map/all_to_all | solution.py:355
  582.1 21.9 %all-to-all-start.6 = ((bf16[8,128,128]{2,1,0:T(8,128)(2,1)}), bf16[8,128,128]{2,1,0:T(8,128)(2,1)S(1)}, u32[]{:S(2)}, u32[]{:S(2)}) async-start(bf16[8,128,128]{2,1,0:T(8,128)(2,1)} %bitcast.78), calls=%async_computation.6 | async-start | bytes 524288 | tf_op jit(solution)/shard_map/all_to_all | solution.py:353
  604.7 31.2 %all-to-all-start.5 = ((bf16[8,128,1024]{1,2,0:T(8,128)(2,1)}), bf16[8,128,1024]{1,2,0:T(8,128)(2,1)S(1)}, u32[]{:S(2)}, u32[]{:S(2)}) async-start(bf16[8,128,1024]{1,2,0:T(8,128)(2,1)} %copy.256), calls=%async_computation.5 | async-start | bytes 4194304 | tf_op jit(solution)/shard_map/all_to_all | solution.py:352
  (29 other events, 233.7 us)
Sparse Core Ops, SparseCore 0:
  76.5 56.9 all-gather.14
  138.5 90.3 all-gather.12
  289.3 35.6 all-gather.10
  526.5 34.7 all-gather.8
